TPU v7x, 32 devices: a whole 2x2x4 slice. The times are simulated.
32 devices in a mesh: dp: 8 (over z, core), seq: 4 (over y, x).
Axes of the slice: x: 2, y: 2, z: 4, core: 2. Of those that a mesh axis runs over, the one named last changes fastest.
Arguments:
- tokens_in: bfloat16 [16384, 1024], P(('dp', 'seq')), may hold values from -6 to 6
- norm_attn: bfloat16 [1024], P('dp'), may hold values from 0.5 to 1.5
- w_query: bfloat16 [1024, 1024], P('dp'), may hold values from -0.1875 to 0.1875
- key_value_weight: bfloat16 [1024, 1024], P('dp'), may hold values from -0.1875 to 0.1875
- gain_query: bfloat16 [64], P('dp'), may hold values from 1 to 2
- gain_key: bfloat16 [64], P('dp'), may hold values from 1 to 2
- w_out: bfloat16 [1024, 1024], P('dp'), may hold values from -0.75 to 0.75
- norm_ffn: bfloat16 [1024], P('dp'), may hold values from 0.5 to 1.5
- w_gate: bfloat16 [1024, 4608], P(None, 'dp'), may hold values from -0.1875 to 0.1875
- w_up: bfloat16 [1024, 4608], P(None, 'dp'), may hold values from -0.1875 to 0.1875
- w_down: bfloat16 [4608, 1024], P('dp'), may hold values from -0.09375 to 0.09375
- cotangent: bfloat16 [16384, 1024], P(('dp', 'seq')), may hold values from -6 to 6
- segments: int32 [8, 2048], P('dp'), may hold values from 0 to 3, never falling along the last dimension, each value on 1 to 1024 neighbouring positions
- blocks: int32 [8, 16], P('dp'), may hold values from 0 to 15, each once within a row
Outputs:
- output: bfloat16 [16384, 1024], P(('dp', 'seq'))
- grad_tokens: float32 [16384, 1024], P(('dp', 'seq'))
- grad_norm_attn: float32 [1024], P('dp')
- grad_w_query: float32 [1024, 1024], P('dp')
- grad_w_keyval: float32 [1024, 1024], P('dp')
- grad_gain_query: float32 [64], P('dp')
- grad_gain_key: float32 [64], P('dp')
- grad_w_out: float32 [1024, 1024], P('dp')
- grad_norm_ffn: float32 [1024], P('dp')
- grad_w_gate: float32 [1024, 4608], P(None, 'dp')
- grad_w_up: float32 [1024, 4608], P(None, 'dp')
- grad_w_down: float32 [4608, 1024], P('dp')
Inputs may be any that keep to these rules, and one draw needn't show every extreme that they name: `segments`: in each row the document numbers never fall, all 4 documents occur, each covers 1 to 1024 places and the longest exactly 1024. `blocks`: each row holds every block number once.
All inputs are finite; a program needn't handle non-finite values.
Results may differ from a plain program's by a relative error of at most 0.025.
Values may be sent and summed in bfloat16 or wider, within the bound.
A program may use at most 192 MiB of HBM per device.

v0:
```python
import math
import jax
import jax.numpy as jnp
from jax import lax
from jax.sharding import PartitionSpec as P

QUERY_HEADS = 16
KEY_VALUE_HEADS = 8
HEAD_SIZE = 64
BLOCK = 128
QUERY_ROWS = 512
EPS = 1e-05
THETA = 1000000.0
MASKED = -1e30


def normed(tensor, gain_vec):
    factor = lax.rsqrt(jnp.mean(tensor * tensor, axis=-1, keepdims=True) + EPS)
    return tensor * factor * gain_vec


def norm_back(tensor, gain_vec, upstream):
    factor = lax.rsqrt(jnp.mean(tensor * tensor, axis=-1, keepdims=True) + EPS)
    unit_value = tensor * factor
    weighted = upstream * gain_vec
    grad_in = factor * (
        weighted - unit_value * jnp.mean(weighted * unit_value, axis=-1, keepdims=True)
    )
    return (grad_in, upstream * unit_value)


def rotate(tensor, angle_cos, angle_sin):
    half_dim = tensor.shape[-1] // 2
    front_half = tensor[..., :half_dim]
    back_half = tensor[..., half_dim:]
    return jnp.concatenate(
        [
            front_half * angle_cos - back_half * angle_sin,
            back_half * angle_cos + front_half * angle_sin,
        ],
        axis=-1,
    )


def angles(offsets, head_dim):
    half_dim = head_dim // 2
    frequency = jnp.exp(
        jnp.arange(half_dim, dtype=jnp.float32) * (-2.0 * math.log(THETA) / head_dim)
    )
    turned = offsets.astype(jnp.float32)[:, None] * frequency[None, :]
    return (jnp.cos(turned)[:, None, :], jnp.sin(turned)[:, None, :])


def layout(segment_row, order_row, block_len):
    length_all = segment_row.shape[0]
    places = jnp.arange(length_all, dtype=jnp.int32)
    seg_start = jnp.concatenate([jnp.ones((1,), dtype=bool), segment_row[1:] != segment_row[:-1]])
    starts = lax.cummax(jnp.where(seg_start, places, 0), axis=0)
    offsets = places - starts
    placed_tokens = (
        order_row[:, None] * block_len + jnp.arange(block_len, dtype=jnp.int32)[None, :]
    ).reshape(length_all)
    return (placed_tokens, segment_row[placed_tokens], offsets[placed_tokens])


def plain_product(left_op, right_op):
    return jnp.dot(left_op, right_op, preferred_element_type=jnp.float32)


def dot_right_t(left_op, right_op):
    return lax.dot_general(
        left_op, right_op, (((1,), (1,)), ((), ())), preferred_element_type=jnp.float32
    )


def dot_left_t(left_op, right_op):
    return lax.dot_general(
        left_op, right_op, (((0,), (0,)), ((), ())), preferred_element_type=jnp.float32
    )


def gate_back(gate_pre, up_pre, upstream):
    gate_sig = jax.nn.sigmoid(gate_pre)
    grad_gate = upstream * up_pre * gate_sig * (1.0 + gate_pre * (1.0 - gate_sig))
    grad_up = upstream * gate_pre * gate_sig
    return (grad_gate.astype(jnp.bfloat16), grad_up.astype(jnp.bfloat16))


def shards(
    tokens_in,
    norm_attn,
    w_query,
    key_value_weight,
    gain_query,
    gain_key,
    w_out,
    norm_ffn,
    w_gate,
    w_up,
    w_down,
    cotangent,
    segments,
    blocks,
):
    sequence_count = lax.axis_size("seq")
    seq_index = lax.axis_index("seq")
    token_rows = tokens_in.shape[0]
    group_rows = token_rows * sequence_count
    local_key_value = KEY_VALUE_HEADS // sequence_count
    repeat_factor = QUERY_HEADS // KEY_VALUE_HEADS
    factor = HEAD_SIZE ** (-0.5)
    count_blocks = group_rows // QUERY_ROWS
    attn_gain, query_w, key_value_matrix, query_gain, key_gain, out_w, ffn_gain = (
        lax.all_gather(norm_attn, "dp", axis=0, tiled=True),
        lax.all_gather(w_query, "dp", axis=0, tiled=True),
        lax.all_gather(key_value_weight, "dp", axis=0, tiled=True),
        lax.all_gather(gain_query, "dp", axis=0, tiled=True),
        lax.all_gather(gain_key, "dp", axis=0, tiled=True),
        lax.all_gather(w_out, "dp", axis=0, tiled=True),
        lax.all_gather(norm_ffn, "dp", axis=0, tiled=True),
    )
    attn_gain = attn_gain.astype(jnp.float32)
    query_gain = query_gain.astype(jnp.float32)
    key_gain = key_gain.astype(jnp.float32)
    ffn_gain = ffn_gain.astype(jnp.float32)
    placed_tokens, documents_for_rows, offsets = layout(segments[0], blocks[0], BLOCK)
    angle_cos, angle_sin = angles(
        lax.dynamic_slice_in_dim(offsets, seq_index * token_rows, token_rows, 0), HEAD_SIZE
    )
    hidden = tokens_in.astype(jnp.float32)
    normalized_input = normed(hidden, attn_gain).astype(jnp.bfloat16)
    query_raw = plain_product(normalized_input, query_w).reshape(token_rows, QUERY_HEADS, HEAD_SIZE)
    key_value_unrotated = plain_product(normalized_input, key_value_matrix).reshape(
        token_rows, KEY_VALUE_HEADS, 2, HEAD_SIZE
    )
    query_low = rotate(normed(query_raw, query_gain), angle_cos, angle_sin).astype(jnp.bfloat16)
    key_low = rotate(normed(key_value_unrotated[:, :, 0], key_gain), angle_cos, angle_sin).astype(
        jnp.bfloat16
    )
    key_value_reduced = jnp.stack(
        [key_low, key_value_unrotated[:, :, 1].astype(jnp.bfloat16)], axis=2
    )
    query_heads, keyval_heads = (
        lax.all_to_all(
            query_low.reshape(token_rows, QUERY_HEADS * HEAD_SIZE),
            "seq",
            split_axis=1,
            concat_axis=0,
            tiled=True,
        ),
        lax.all_to_all(
            key_value_reduced.reshape(token_rows, KEY_VALUE_HEADS * 2 * HEAD_SIZE),
            "seq",
            split_axis=1,
            concat_axis=0,
            tiled=True,
        ),
    )
    query_matrix = query_heads.reshape(group_rows, local_key_value, repeat_factor, HEAD_SIZE)
    keyval_group = keyval_heads.reshape(group_rows, local_key_value, 2, HEAD_SIZE)
    key_rows = keyval_group[:, :, 0]
    value_rows = keyval_group[:, :, 1]

    def scores_of(block_idx):
        row_start = block_idx * QUERY_ROWS
        query_rows = lax.dynamic_slice_in_dim(query_matrix, row_start, QUERY_ROWS, 0)
        placed_rows = lax.dynamic_slice_in_dim(placed_tokens, row_start, QUERY_ROWS, 0)
        docs_rows = lax.dynamic_slice_in_dim(documents_for_rows, row_start, QUERY_ROWS, 0)
        allowed = (docs_rows[:, None] == documents_for_rows[None, :]) & (
            placed_tokens[None, :] <= placed_rows[:, None]
        )
        raw_scores = (
            jnp.einsum("rkad,jkd->karj", query_rows, key_rows, preferred_element_type=jnp.float32)
            * factor
        )
        return (query_rows, jnp.where(allowed, raw_scores, MASKED))

    def forward_block(block_idx):
        query_rows, masked = scores_of(block_idx)
        row_top = jnp.max(masked, axis=-1, keepdims=True)
        row_total = jnp.sum(jnp.exp(masked - row_top), axis=-1, keepdims=True)
        log_total = row_top + jnp.log(row_total)
        weights_low = jnp.exp(masked - log_total).astype(jnp.bfloat16)
        block_result = jnp.einsum(
            "karj,jkd->rkad", weights_low, value_rows, preferred_element_type=jnp.float32
        )
        return (block_result.astype(jnp.bfloat16), log_total)

    head_outs, log_totals = lax.map(forward_block, jnp.arange(count_blocks))
    attended = lax.all_to_all(
        head_outs.reshape(group_rows, local_key_value * repeat_factor * HEAD_SIZE),
        "seq",
        split_axis=0,
        concat_axis=1,
        tiled=True,
    )
    middle = hidden + plain_product(attended, out_w)
    ffn_in = normed(middle, ffn_gain).astype(jnp.bfloat16)
    gate_all, up_all, down_all = (
        lax.all_gather(w_gate, "dp", axis=1, tiled=True),
        lax.all_gather(w_up, "dp", axis=1, tiled=True),
        lax.all_gather(w_down, "dp", axis=0, tiled=True),
    )
    gate_pre = plain_product(ffn_in, gate_all)
    up_pre = plain_product(ffn_in, up_all)
    activated = (jax.nn.silu(gate_pre) * up_pre).astype(jnp.bfloat16)
    ffn_result = plain_product(activated, down_all)
    block_output = (middle + ffn_result).astype(jnp.bfloat16)
    upstream = cotangent.astype(jnp.float32)
    grad_act = dot_right_t(cotangent, down_all)
    grad_down_part = dot_left_t(activated, cotangent)
    grad_gate, grad_up = gate_back(gate_pre, up_pre, grad_act)
    grad_gate_part = dot_left_t(ffn_in, grad_gate)
    grad_up_part = dot_left_t(ffn_in, grad_up)
    grad_ffn_in = dot_right_t(grad_gate, gate_all) + dot_right_t(grad_up, up_all)
    grad_gate_w, grad_up_w, grad_down = (
        lax.psum_scatter(
            grad_gate_part.astype(jnp.bfloat16), "dp", scatter_dimension=1, tiled=True
        ).astype(jnp.float32),
        lax.psum_scatter(
            grad_up_part.astype(jnp.bfloat16), "dp", scatter_dimension=1, tiled=True
        ).astype(jnp.float32),
        lax.psum_scatter(
            grad_down_part.astype(jnp.bfloat16), "dp", scatter_dimension=0, tiled=True
        ).astype(jnp.float32),
    )
    grad_middle_add, ffn_gain_terms = norm_back(middle, ffn_gain, grad_ffn_in)
    grad_ffn_gain = jnp.sum(ffn_gain_terms, axis=0)
    grad_middle = upstream + grad_middle_add
    grad_branch = grad_middle.astype(jnp.bfloat16)
    grad_out_w = dot_left_t(attended, grad_branch)
    grad_attended = dot_right_t(grad_branch, out_w).astype(jnp.bfloat16)
    grad_head_outs = lax.all_to_all(grad_attended, "seq", split_axis=1, concat_axis=0, tiled=True)
    grad_outs_all = grad_head_outs.reshape(group_rows, local_key_value, repeat_factor, HEAD_SIZE)

    def backward_block(carried, group_members):
        grad_keys, grad_values = carried
        block_idx, log_total = group_members
        query_rows, masked = scores_of(block_idx)
        weights_full = jnp.exp(masked - log_total)
        weights_low = weights_full.astype(jnp.bfloat16)
        grad_rows = lax.dynamic_slice_in_dim(grad_outs_all, block_idx * QUERY_ROWS, QUERY_ROWS, 0)
        grad_weights = jnp.einsum(
            "rkad,jkd->karj", grad_rows, value_rows, preferred_element_type=jnp.float32
        )
        row_dot = jnp.sum(weights_full * grad_weights, axis=-1, keepdims=True)
        grad_scores = (weights_full * (grad_weights - row_dot)).astype(jnp.bfloat16)
        grad_query_rows = (
            jnp.einsum("karj,jkd->rkad", grad_scores, key_rows, preferred_element_type=jnp.float32)
            * factor
        )
        grad_keys = (
            grad_keys
            + jnp.einsum(
                "karj,rkad->jkd", grad_scores, query_rows, preferred_element_type=jnp.float32
            )
            * factor
        )
        grad_values = grad_values + jnp.einsum(
            "karj,rkad->jkd", weights_low, grad_rows, preferred_element_type=jnp.float32
        )
        return ((grad_keys, grad_values), grad_query_rows.astype(jnp.bfloat16))

    zero_heads = jnp.zeros((group_rows, local_key_value, HEAD_SIZE), jnp.float32)
    (grad_keys, grad_values), grad_query_blocks = lax.scan(
        backward_block, (zero_heads, zero_heads), (jnp.arange(count_blocks), log_totals)
    )
    grad_query_heads = grad_query_blocks.reshape(
        group_rows, local_key_value * repeat_factor * HEAD_SIZE
    )
    grad_keyval_heads = (
        jnp.stack([grad_keys, grad_values], axis=2)
        .astype(jnp.bfloat16)
        .reshape(group_rows, local_key_value * 2 * HEAD_SIZE)
    )
    grad_query_tok, key_value_gradient_tokens = (
        lax.all_to_all(grad_query_heads, "seq", split_axis=0, concat_axis=1, tiled=True),
        lax.all_to_all(grad_keyval_heads, "seq", split_axis=0, concat_axis=1, tiled=True),
    )
    grad_query_rot = rotate(
        grad_query_tok.reshape(token_rows, QUERY_HEADS, HEAD_SIZE).astype(jnp.float32),
        angle_cos,
        -angle_sin,
    )
    grad_query_raw, query_gain_terms = norm_back(query_raw, query_gain, grad_query_rot)
    grad_query_gain = jnp.sum(query_gain_terms, axis=(0, 1))
    key_value_gradient_split = key_value_gradient_tokens.reshape(
        token_rows, KEY_VALUE_HEADS, 2, HEAD_SIZE
    )
    grad_key_rot = rotate(
        key_value_gradient_split[:, :, 0].astype(jnp.float32), angle_cos, -angle_sin
    )
    grad_key_raw, key_gain_terms = norm_back(key_value_unrotated[:, :, 0], key_gain, grad_key_rot)
    grad_key_gain = jnp.sum(key_gain_terms, axis=(0, 1))
    grad_query_low = grad_query_raw.astype(jnp.bfloat16).reshape(
        token_rows, QUERY_HEADS * HEAD_SIZE
    )
    grad_keyval_low = jnp.stack(
        [grad_key_raw.astype(jnp.bfloat16), key_value_gradient_split[:, :, 1]], axis=2
    ).reshape(token_rows, KEY_VALUE_HEADS * 2 * HEAD_SIZE)
    grad_normed_in = dot_right_t(grad_query_low, query_w) + dot_right_t(
        grad_keyval_low, key_value_matrix
    )
    grad_query_w = dot_left_t(normalized_input, grad_query_low)
    grad_keyval_w = dot_left_t(normalized_input, grad_keyval_low)
    grad_hidden_add, attn_gain_terms = norm_back(hidden, attn_gain, grad_normed_in)
    grad_attn_gain = jnp.sum(attn_gain_terms, axis=0)
    grad_hidden = grad_middle + grad_hidden_add
    (
        owned_attn_gain,
        owned_query_w,
        owned_keyval_w,
        owned_query_gain,
        owned_key_gain,
        owned_out_w,
        owned_ffn_gain,
    ) = (
        lax.psum_scatter(
            grad_attn_gain.astype(jnp.bfloat16), "dp", scatter_dimension=0, tiled=True
        ).astype(jnp.float32),
        lax.psum_scatter(
            grad_query_w.astype(jnp.bfloat16), "dp", scatter_dimension=0, tiled=True
        ).astype(jnp.float32),
        lax.psum_scatter(
            grad_keyval_w.astype(jnp.bfloat16), "dp", scatter_dimension=0, tiled=True
        ).astype(jnp.float32),
        lax.psum_scatter(
            grad_query_gain.astype(jnp.bfloat16), "dp", scatter_dimension=0, tiled=True
        ).astype(jnp.float32),
        lax.psum_scatter(
            grad_key_gain.astype(jnp.bfloat16), "dp", scatter_dimension=0, tiled=True
        ).astype(jnp.float32),
        lax.psum_scatter(
            grad_out_w.astype(jnp.bfloat16), "dp", scatter_dimension=0, tiled=True
        ).astype(jnp.float32),
        lax.psum_scatter(
            grad_ffn_gain.astype(jnp.bfloat16), "dp", scatter_dimension=0, tiled=True
        ).astype(jnp.float32),
    )
    (
        total_attn_gain,
        total_query_w,
        total_keyval_w,
        total_query_gain,
        total_key_gain,
        total_out_w,
        total_ffn_gain,
        total_gate_w,
        total_up_w,
        total_down_w,
    ) = lax.psum(
        (
            owned_attn_gain,
            owned_query_w,
            owned_keyval_w,
            owned_query_gain,
            owned_key_gain,
            owned_out_w,
            owned_ffn_gain,
            grad_gate_w,
            grad_up_w,
            grad_down,
        ),
        "seq",
    )
    return (
        block_output,
        grad_hidden,
        total_attn_gain,
        total_query_w,
        total_keyval_w,
        total_query_gain,
        total_key_gain,
        total_out_w,
        total_ffn_gain,
        total_gate_w,
        total_up_w,
        total_down_w,
    )


def solution(mesh):
    return jax.shard_map(
        shards,
        mesh=mesh,
        in_specs=(
            P(("dp", "seq"), None),
            P("dp"),
            P("dp", None),
            P("dp", None),
            P("dp"),
            P("dp"),
            P("dp", None),
            P("dp"),
            P(None, "dp"),
            P(None, "dp"),
            P("dp", None),
            P(("dp", "seq"), None),
            P("dp", None),
            P("dp", None),
        ),
        out_specs=(
            P(("dp", "seq"), None),
            P(("dp", "seq"), None),
            P("dp"),
            P("dp", None),
            P("dp", None),
            P("dp"),
            P("dp"),
            P("dp", None),
            P("dp"),
            P(None, "dp"),
            P(None, "dp"),
            P("dp", None),
        ),
        check_vma=False,
    )
```

profile of v0, /device:TPU:8, one launch (start us, length us, event | category | flops | bytes accessed | tf_op | source)
XLA Modules:
  0.0 1338.1 jit_solution(3187364560856251971)
XLA Ops:
  11.2 9.0 all-gather
  22.0 14.6 %all-reduce.8 = (bf16[64]{0:T(256)(128)(2,1)S(1)}, bf16[64]{0:T(256)(128)(2,1)S(1)}) all-reduce(bf16[64]{0:T(256)(128)(2,1)S(1)} %dynamic-update-slice, bf16[64]{0:T(256)(128)(2,1)S(1)} %dynamic-update-slice.1), channel_id=1, replica_groups=mesh['dp'=8,'seq'=4] {'dp'}, use_global_device_ids=true, to_apply=%add | all-reduce | flops 128 | bytes 512
  37.3 11.8 gather_fusion.1
  50.4 4.2 fusion.90
  59.4 3.6 all-to-all-start
  63.0 7.5 all-gather.11.cloned.1.call-done
  76.1 3.6 all-to-all-start.1
  80.3 11.8 gather_fusion
  102.5 61.7 %while.28 = (s32[]{:T(128)}, bf16[4,512,2,2,64]{1,4,3,2,0:T(8,128)(2,1)}, f32[4,2,2,512,1]{3,2,1,4,0:T(2,128)}, s32[4]{0:T(128)S(1)}, s32[2048]{0:T(1024)S(1)}, ...) while((s32[]{:T(128)}, ...), condition=%wide.region_8.9_spmd.clone, body=%wide.region_5.8_spmd.clone.sunk | while | flops 1123155968 | bytes 56201496 | solution.py:189
  108.0 4.3 fusion.149
  112.9 5.0 fusion.150
  123.4 4.3 fusion.149
  128.3 5.0 fusion.150
  138.8 4.3 fusion.149
  143.8 5.0 fusion.150
  154.3 4.3 fusion.149
  159.2 5.0 fusion.150
  164.2 4.4 all-to-all-start.2
  168.6 12.5 all-gather.1
  182.9 3.5 multiply_reduce_fusion.4
  189.8 10.1 fusion.93
  199.9 80.6 %all-gather.17.cloned.1.call-done = bf16[1024,4608]{0,1:T(8,128)(2,1)} async-done(((bf16[1024,576]{0,1:T(8,128)(2,1)}), bf16[1024,4608]{0,1:T(8,128)(2,1)}) %all-gather.17.cloned.1.call-update) | async-done | bytes 9437200 | tf_op jit(solution)/shard_map/all_gather | solution.py:201
  280.5 10.2 fusion.94
  290.7 80.5 %all-gather.19.cloned.1.call-done = bf16[4608,1024]{1,0:T(8,128)(2,1)} async-done(((bf16[576,1024]{1,0:T(8,128)(2,1)}), bf16[4608,1024]{1,0:T(8,128)(2,1)}) %all-gather.19.cloned.1.call-update) | async-done | bytes 9437200 | tf_op jit(solution)/shard_map/all_gather | solution.py:202
  371.2 18.5 %multiply_convert_fusion = (bf16[512,4608]{1,0:T(8,128)(2,1)}, bf16[512,4608]{1,0:T(8,128)(2,1)}, bf16[512,4608]{1,0:T(8,128)(2,1)}) fusion(f32[512,4608]{1,0:T(8,128)} %fusion.93, f32[512,4608]{1,0:T(8,128)} %fusion.94, bf16[512,1024]{1,0:T(8,128)(2,1)} %param.29, bf16[4608,1024]{1,0:T(8,128)(2,1)} %all-gather.19.cloned.1.call-done), kind=kOutput, calls=%fused_computation.69 | convolution fusion | flops 4869586944 | bytes 43515904 | tf_op jit(solution)/shard_map/dot_general | solution.py:71
  389.7 9.6 fusion.95
  399.4 5.9 multiply_reduce_fusion
  409.3 4.3 all-to-all-start.3
  413.7 4.5 convolution_convert_fusion.3
  418.2 9.8 all-to-all-done.3
  434.4 199.1 %while.29 = (s32[]{:T(128)}, f32[2048,2,64]{0,2,1:T(8,128)}, f32[2048,2,64]{0,2,1:T(8,128)}, bf16[4,512,2,2,64]{1,4,3,2,0:T(8,128)(2,1)}, s32[4]{0:T(128)S(1)}, ...) while((s32[]{:T(128)}, f32[2048,2,64]{0,2,1:T(8,128)}, ...), condition=%wide.region_13.14_spmd.clone, body=%wide.region_11.13_spmd.clone.sunk | while | flops 2751987712 | bytes 254768080 | solution.py:265
  442.1 11.6 fusion.160
  453.6 10.9 fusion.161
  464.5 6.2 fusion.162
  470.7 8.4 fusion.163
  479.2 4.8 fusion.164
  491.6 11.5 fusion.160
  503.1 10.9 fusion.161
  514.0 6.4 fusion.162
  520.4 8.4 fusion.163
  528.9 4.8 fusion.164
  541.3 11.5 fusion.160
  552.8 10.9 fusion.161
  563.7 6.4 fusion.162
  570.1 8.4 fusion.163
  578.6 4.8 fusion.164
  591.0 11.5 fusion.160
  602.6 10.9 fusion.161
  613.5 6.4 fusion.162
  619.9 8.4 fusion.163
  628.3 4.8 fusion.164
  633.5 3.7 all-to-all-start.4
  639.4 11.2 all-to-all-done.4
  657.2 4.6 multiply_reduce_fusion.1
  668.3 16.0 %all_to_all.90 = bf16[4,512,256]{1,2,0:T(8,128)(2,1)S(1)} all-to-all(bf16[4,512,256]{1,2,0:T(8,128)(2,1)S(1)} %copy.108), channel_id=1, replica_groups=mesh['dp'=8,'seq'=4] {'seq'}, dimensions={0} | all-to-all | bytes 2097152 | tf_op jit(solution)/shard_map/all_to_all | solution.py:278
  691.9 10.0 convolution_convert_fusion.2
  702.0 10.2 convolution_convert_fusion.1
  713.4 10.0 convolution_convert_fusion
  725.0 9.9 add_convert_fusion
  741.4 13.4 %all-reduce.7 = (bf16[1024]{0:T(1024)(128)(2,1)S(1)}, bf16[64]{0:T(256)(128)(2,1)S(1)}, bf16[64]{0:T(256)(128)(2,1)S(1)}, bf16[1024]{0:T(1024)(128)(2,1)S(1)}) all-reduce(bf16[1024]{0:T(1024)(128)(2,1)S(1)} %get-tuple-element.224, bf16[64]{0:T(256)(128)(2,1)S(1)} %reduce_sum.160, ...), channel_id=2, replica_groups=mesh['dp'=8,'seq'=4] {'dp'}, use_global_device_ids=true, to_apply=%region_18.19.clone | all-reduce | flops 2176 | bytes 8704
  758.6 78.1 %reduce-scatter.13.cloned.1.call-done = bf16[1024,576]{0,1:T(8,128)(2,1)} async-done(((bf16[1024,4608]{0,1:T(8,128)(2,1)}), bf16[1024,576]{0,1:T(8,128)(2,1)}) %reduce-scatter.13.cloned.1.call-update) | async-done | bytes 1179664 | tf_op jit(solution)/shard_map/reduce_scatter | solution.py:217
  836.7 99.8 %reduce-scatter.15.cloned.1.call-done = bf16[1024,576]{0,1:T(8,128)(2,1)} async-done(((bf16[1024,4608]{0,1:T(8,128)(2,1)}), bf16[1024,576]{0,1:T(8,128)(2,1)}) %reduce-scatter.15.cloned.1.call-update) | async-done | bytes 1179664 | tf_op jit(solution)/shard_map/reduce_scatter | solution.py:220
  936.5 100.1 %reduce-scatter.17.cloned.1.call-done = bf16[576,1024]{1,0:T(8,128)(2,1)} async-done(((bf16[4608,1024]{1,0:T(8,128)(2,1)}), bf16[576,1024]{1,0:T(8,128)(2,1)}) %reduce-scatter.17.cloned.1.call-update) | async-done | bytes 1179664 | tf_op jit(solution)/shard_map/reduce_scatter | solution.py:223
  1036.6 294.2 %all-reduce.10 = (f32[128]{0:T(128)}, f32[128,1024]{1,0:T(8,128)}, f32[128,1024]{1,0:T(8,128)}, f32[8]{0:T(128)}, f32[8]{0:T(128)}, /*index=5*/f32[128,1024]{1,0...) all-reduce(f32[128]{0:T(128)S(1)} %dynamic-slice_convert_fusion.4, ...), channel_id=1, replica_groups=mesh['dp'=8,'seq'=4] {'seq'}, use_global_device_ids=true, to_apply=%region_19.20 | all-reduce | flops 2162960 | bytes 12978304 | tf_op jit(solution)/shard_map/psum | solution.py:351
  (416 shorter events, 127.0 us)
Async XLA Ops:
  7.2 13.1 copy-start.48
  7.2 14.3 %copy-start.56 = (bf16[8]{0:T(256)(128)(2,1)S(1)}, bf16[8]{0:T(256)(128)(2,1)}, u32[]{:S(2)}) copy-start(bf16[8]{0:T(256)(128)(2,1)} %param.22) | copy-start | bytes 52
  7.2 14.6 %copy-start.57 = (bf16[8]{0:T(256)(128)(2,1)S(1)}, bf16[8]{0:T(256)(128)(2,1)}, u32[]{:S(2)}) copy-start(bf16[8]{0:T(256)(128)(2,1)} %param.23) | copy-start | bytes 52
  7.2 29.9 %copy-start.58 = (s32[1,16]{1,0:T(1,128)S(1)}, s32[1,16]{1,0:T(1,128)}, u32[]{:S(2)}) copy-start(s32[1,16]{1,0:T(1,128)} %param.31) | copy-start | bytes 196
  7.2 43.2 %all-gather.9.cloned.1.call-start = ((), (), s32[]{:S(2)}) async-start(), calls=%async_computation.12 | async-start | bytes 2359296 | tf_op jit(solution)/shard_map/all_gather | solution.py:115
  8.0 62.5 %all-gather.11.cloned.1.call-start = ((), (), s32[]{:S(2)}) async-start(), calls=%async_computation.13 | async-start | bytes 2359296 | tf_op jit(solution)/shard_map/all_gather | solution.py:116
  8.7 172.4 %all-gather.13.cloned.1.call-start = ((), (), s32[]{:S(2)}) async-start(), calls=%async_computation.14 | async-start | bytes 2359296 | tf_op jit(solution)/shard_map/all_gather | solution.py:119
  9.5 180.3 %all-gather.15.cloned.1.call-start = ((), (), s32[]{:S(2)}) async-start(), calls=%async_computation.15 | async-start | bytes 10616832 | tf_op jit(solution)/shard_map/all_gather | solution.py:200
  10.0 270.4 %all-gather.17.cloned.1.call-start = ((), (), s32[]{:S(2)}) async-start(), calls=%async_computation.16 | async-start | bytes 10616832 | tf_op jit(solution)/shard_map/all_gather | solution.py:201
  20.3 50.2 %copy-start.40 = (f32[8,1,128]{2,1,0:T(1,128)}, f32[8,1,128]{2,1,0:T(1,128)S(1)}, u32[]{:S(2)}) copy-start(f32[8,1,128]{2,1,0:T(1,128)S(1)} %convert_element_type.218) | copy-start | bytes 12292
  36.6 20.3 %copy-start.46 = (f32[64]{0:T(128)}, f32[64]{0:T(128)S(1)}, u32[]{:S(2)}) copy-start(f32[64]{0:T(128)S(1)} %convert_element_type.174) | copy-start | bytes 772
  36.7 37.1 %copy-start.44 = (f32[64]{0:T(128)}, f32[64]{0:T(128)S(1)}, u32[]{:S(2)}) copy-start(f32[64]{0:T(128)S(1)} %convert_element_type.177) | copy-start | bytes 772
  37.3 11.9 copy-start.16
  49.5 21.0 %copy-start.42 = (f32[512]{0:T(512)}, f32[512]{0:T(512)S(1)}, u32[]{:S(2)}) copy-start(f32[512]{0:T(512)S(1)} %add_rsqrt_fusion.3) | copy-start | bytes 6148
  50.4 24.4 %copy-start.21 = (f32[512,32]{0,1:T(8,128)}, f32[512,32]{0,1:T(8,128)S(1)}, u32[]{:S(2)}) copy-start(f32[512,32]{0,1:T(8,128)S(1)} %get-tuple-element.315) | copy-start | bytes 196612
  59.4 16.7 %all-to-all-start = ((bf16[512,4,256]{0,2,1:T(8,128)(2,1)}), bf16[512,4,256]{0,2,1:T(8,128)(2,1)S(1)}, u32[]{:S(2)}, u32[]{:S(2)}) async-start(bf16[512,4,256]{0,2,1:T(8,128)(2,1)} %bitcast.11), calls=%async_computation | async-start | bytes 2097152 | tf_op jit(solution)/shard_map/all_to_all | solution.py:144
  76.1 19.6 %all-to-all-start.1 = ((bf16[512,4,256]{0,2,1:T(8,128)(2,1)}), bf16[512,4,256]{0,2,1:T(8,128)(2,1)S(1)}, u32[]{:S(2)}, u32[]{:S(2)}) async-start(bf16[512,4,256]{0,2,1:T(8,128)(2,1)} %bitcast.17), calls=%async_computation.1 | async-start | bytes 2097152 | tf_op jit(solution)/shard_map/all_to_all | solution.py:151
  79.8 291.4 %all-gather.19.cloned.1.call-start = ((), (), s32[]{:S(2)}) async-start(), calls=%async_computation.17 | async-start | bytes 10616832 | tf_op jit(solution)/shard_map/all_gather | solution.py:202
  164.2 18.7 %all-to-all-start.2 = ((bf16[4,512,256]{1,2,0:T(8,128)(2,1)}), bf16[4,512,256]{1,2,0:T(8,128)(2,1)}, u32[]{:S(2)}, u32[]{:S(2)}) async-start(bf16[4,512,256]{1,2,0:T(8,128)(2,1)} %bitcast.312), calls=%async_computation.2 | async-start | bytes 2097152 | tf_op jit(solution)/shard_map/all_to_all | solution.py:190
  389.7 9.6 copy-start.10
  389.7 9.6 copy-start.54
  389.7 9.8 copy-start.61
  399.4 5.9 copy-start.30
  409.3 18.7 %all-to-all-start.3 = ((bf16[512,4,256]{2,0,1:T(8,128)(2,1)}), bf16[512,4,256]{2,0,1:T(8,128)(2,1)}, u32[]{:S(2)}, u32[]{:S(2)}) async-start(bf16[512,4,256]{2,0,1:T(8,128)(2,1)} %bitcast.310), calls=%async_computation.3 | async-start | bytes 2097152 | tf_op jit(solution)/shard_map/all_to_all | solution.py:233
  413.6 345.0 %reduce-scatter.11.cloned.1.call-start = ((), (), s32[]{:S(2)}) async-start(), calls=%async_computation.20 | async-start | bytes 2359296 | tf_op jit(solution)/shard_map/reduce_scatter | solution.py:333
  434.6 5.7 copy-start.38
  434.6 5.8 copy-start.23
  439.4 14.2 %copy-start.1 = (f32[2,512,2,2048]{3,1,2,0:T(8,128)}, f32[2,512,2,2048]{3,1,2,0:T(8,128)S(1)}, u32[]{:S(2)}) copy-start(f32[2,512,2,2048]{3,1,2,0:T(8,128)S(1)} %fusion.159) | copy-start | bytes 50331652 | tf_op jit(solution)/shard_map/while
  464.5 6.2 copy-start.25
  464.5 14.6 %slice-start = ((s8[8388608]{0:T(1024)(128)(4,1)}), s8[4194304]{0:T(1024)(128)(4,1)S(1)}, s32[]{:S(2)}) async-start(s8[8388608]{0:T(1024)(128)(4,1)} %bitcast.295), calls=%async_computation.24 | async-start | bytes 8388608 | tf_op jit(solution)/shard_map/while
  470.7 8.4 slice-start.1
  479.1 4.9 copy-start.26
  484.1 5.7 copy-start.38
  484.1 5.8 copy-start.23
  488.9 14.2 %copy-start.1 = (f32[2,512,2,2048]{3,1,2,0:T(8,128)}, f32[2,512,2,2048]{3,1,2,0:T(8,128)S(1)}, u32[]{:S(2)}) copy-start(f32[2,512,2,2048]{3,1,2,0:T(8,128)S(1)} %fusion.159) | copy-start | bytes 50331652 | tf_op jit(solution)/shard_map/while
  514.0 6.4 copy-start.25
  514.0 14.8 %slice-start = ((s8[8388608]{0:T(1024)(128)(4,1)}), s8[4194304]{0:T(1024)(128)(4,1)S(1)}, s32[]{:S(2)}) async-start(s8[8388608]{0:T(1024)(128)(4,1)} %bitcast.295), calls=%async_computation.24 | async-start | bytes 8388608 | tf_op jit(solution)/shard_map/while
  520.4 8.4 slice-start.1
  533.8 5.7 copy-start.38
  533.8 5.8 copy-start.23
  538.7 14.2 %copy-start.1 = (f32[2,512,2,2048]{3,1,2,0:T(8,128)}, f32[2,512,2,2048]{3,1,2,0:T(8,128)S(1)}, u32[]{:S(2)}) copy-start(f32[2,512,2,2048]{3,1,2,0:T(8,128)S(1)} %fusion.159) | copy-start | bytes 50331652 | tf_op jit(solution)/shard_map/while
  563.7 6.4 copy-start.25
  563.7 14.8 %slice-start = ((s8[8388608]{0:T(1024)(128)(4,1)}), s8[4194304]{0:T(1024)(128)(4,1)S(1)}, s32[]{:S(2)}) async-start(s8[8388608]{0:T(1024)(128)(4,1)} %bitcast.295), calls=%async_computation.24 | async-start | bytes 8388608 | tf_op jit(solution)/shard_map/while
  570.1 8.4 slice-start.1
  578.5 4.9 copy-start.26
  583.5 5.7 copy-start.38
  583.5 5.8 copy-start.23
  588.4 14.2 %copy-start.1 = (f32[2,512,2,2048]{3,1,2,0:T(8,128)}, f32[2,512,2,2048]{3,1,2,0:T(8,128)S(1)}, u32[]{:S(2)}) copy-start(f32[2,512,2,2048]{3,1,2,0:T(8,128)S(1)} %fusion.159) | copy-start | bytes 50331652 | tf_op jit(solution)/shard_map/while
  613.5 6.4 copy-start.25
  613.5 14.8 %slice-start = ((s8[8388608]{0:T(1024)(128)(4,1)}), s8[4194304]{0:T(1024)(128)(4,1)S(1)}, s32[]{:S(2)}) async-start(s8[8388608]{0:T(1024)(128)(4,1)} %bitcast.295), calls=%async_computation.24 | async-start | bytes 8388608 | tf_op jit(solution)/shard_map/while
  619.9 8.4 slice-start.1
  628.2 4.9 copy-start.26
  633.5 17.1 %all-to-all-start.4 = ((bf16[4,512,256]{1,2,0:T(8,128)(2,1)}), bf16[4,512,256]{1,2,0:T(8,128)(2,1)S(1)}, u32[]{:S(2)}, u32[]{:S(2)}) async-start(bf16[4,512,256]{1,2,0:T(8,128)(2,1)} %bitcast.311), calls=%async_computation.4 | async-start | bytes 2097152 | tf_op jit(solution)/shard_map/all_to_all | solution.py:277
  637.1 121.5 %reduce-scatter.7.cloned.1.call-start = ((), (), s32[]{:S(2)}) async-start(), calls=%async_computation.18 | async-start | bytes 2359296 | tf_op jit(solution)/shard_map/reduce_scatter | solution.py:321
  639.4 11.5 copy-start.22
  639.4 11.5 copy-start.33
  657.2 5.6 copy-start.17
  657.2 5.6 copy-start.41
  657.2 5.6 copy-start.43
  665.5 93.1 %reduce-scatter.9.cloned.1.call-start = ((), (), s32[]{:S(2)}) async-start(), calls=%async_computation.19 | async-start | bytes 2359296 | tf_op jit(solution)/shard_map/reduce_scatter | solution.py:324
  690.7 146.0 %reduce-scatter.13.cloned.1.call-start = ((), (), s32[]{:S(2)}) async-start(), calls=%async_computation.21 | async-start | bytes 10616832 | tf_op jit(solution)/shard_map/reduce_scatter | solution.py:217
  702.0 234.6 %reduce-scatter.15.cloned.1.call-start = ((), (), s32[]{:S(2)}) async-start(), calls=%async_computation.22 | async-start | bytes 10616832 | tf_op jit(solution)/shard_map/reduce_scatter | solution.py:220
  712.2 324.4 %reduce-scatter.17.cloned.1.call-start = ((), (), s32[]{:S(2)}) async-start(), calls=%async_computation.23 | async-start | bytes 10616832 | tf_op jit(solution)/shard_map/reduce_scatter | solution.py:223
  738.4 16.8 %copy-start.19 = (f32[512,1024]{1,0:T(8,128)S(1)}, f32[512,1024]{1,0:T(8,128)}, u32[]{:S(2)}) copy-start(f32[512,1024]{1,0:T(8,128)} %copy-done.18) | copy-start | bytes 6291460
  (68 other events, 227.0 us)
Sparse Core Ops, SparseCore 0:
  9.7 30.5 all-gather.8
  41.9 28.5 all-gather.10
  72.1 28.5 all-gather.12
  102.2 87.5 all-gather.14
  191.3 89.1 all-gather.16
  282.0 89.1 all-gather.18
  418.3 33.8 reduce-scatter.10
  665.7 32.2 reduce-scatter.6
  700.3 34.5 reduce-scatter.8
  737.0 99.7 reduce-scatter.12
  839.0 97.4 reduce-scatter.14
  938.7 97.8 reduce-scatter.16
where the time goes:
time: 1350 us; the launch traced here: 1340 us
  waiting for transfers between devices  474 us (35%)
  blocking collectives  360 us (27%)
  matrix products  293 us (22%)
  other arithmetic  94.1 us (7%)
  local copies, waits for them, and re-layouts  73.3 us (5%)
  starting transfers between devices  20.2 us (1%)
  between operations  17.5 us (1%)
    psum x1, blocking collectives, shards(): lax.psum((owned_attn_gain, owned_query_w, owned_keyval_w, owned_query_gai...  294 us
    reduce_scatter x1, waiting for transfers between devices, shards(): lax.psum_scatter(grad_down_part.astype(jnp.bfloat16), 'dp', scatter_dimen...  100 us
    reduce_scatter x1, waiting for transfers between devices, shards(): lax.psum_scatter(grad_up_part.astype(jnp.bfloat16), 'dp', scatter_dimensi...  99.8 us
    all_gather x1, waiting for transfers between devices, shards(): lax.all_gather(w_up, 'dp', axis=1, tiled=True)  80.6 us
    all_gather x1, waiting for transfers between devices, shards(): lax.all_gather(w_down, 'dp', axis=0, tiled=True)  80.5 us
    reduce_scatter x1, waiting for transfers between devices, shards(): lax.psum_scatter(grad_gate_part.astype(jnp.bfloat16), 'dp', scatter_dimen...  78.1 us
    dot_general x4, matrix products, backward_block(): jnp.einsum('rkad,jkd->karj', grad_rows, value_rows, preferred_element_typ...  46.1 us
    convert_element_type x4, other arithmetic, backward_block(): grad_scores = (weights_full * (grad_weights - row_dot)).astype(jnp.bfloat16)  43.6 us
  transfers between devices with their start and end apart: 17, of which 10 were waited for; matrix products, arithmetic and copies ran while one was open for 31% of the time, Pallas kernels for 0%

commit v1 on v0

--- a/solution.py
+++ b/solution.py
@@ -196,10 +196,25 @@
     )
     middle = hidden + plain_product(attended, out_w)
     ffn_in = normed(middle, ffn_gain).astype(jnp.bfloat16)
+
+    def list_keys_on_mesh(frame):
+        later = lax.axis_size("dp")
+        small = lax.axis_index("dp")
+        state_now, h_now, out_arr = (later, small, frame.shape[0])
+        prior, o_now = (frame, 1)
+        while o_now < state_now:
+            d_next = lax.ppermute(
+                prior, "dp", [(q, (q - o_now) % state_now) for q in range(state_now)]
+            )
+            prior = jnp.concatenate([prior, d_next], axis=0)
+            o_now = 2 * o_now
+        reply = jnp.roll(prior, h_now * out_arr, 0)
+        return reply
+
     gate_all, up_all, down_all = (
         lax.all_gather(w_gate, "dp", axis=1, tiled=True),
         lax.all_gather(w_up, "dp", axis=1, tiled=True),
-        lax.all_gather(w_down, "dp", axis=0, tiled=True),
+        list_keys_on_mesh(w_down),
     )
     gate_pre = plain_product(ffn_in, gate_all)
     up_pre = plain_product(ffn_in, up_all)

time: 1350 us -> 1550 us (1.15)
  blocking collectives: 360 us -> 569 us
  waiting for transfers between devices: 474 us -> 398 us
  local copies, waits for them, and re-layouts: 73.3 us -> 113 us
    all_gather x1, blocking collectives: 12.5 us -> 196 us  [shards(): lax.all_gather(norm_ffn, 'dp', axis=0, tiled=True)]
    ppermute x0 -> x3, waiting for transfers between devices: none -> 98.4 us  [list_keys_on_mesh(): lax.ppermute(prior, 'dp', [(q, (q - o_now) % state_now) for q in range(st...]
    all_gather x1, waiting for transfers between devices: 80.6 us -> 0.01 us  [shards(): lax.all_gather(w_up, 'dp', axis=1, tiled=True)]
    all_gather x1 -> x0, waiting for transfers between devices: 80.5 us -> none  [shards(): lax.all_gather(w_down, 'dp', axis=0, tiled=True)]
    all_gather x1, blocking collectives: 9 us -> 35.3 us  [shards(): lax.all_gather(norm_attn, 'dp', axis=0, tiled=True)]
  transfers between devices with their start and end apart: 17 -> 19, of which waited for: 10 -> 7; matrix products, arithmetic and copies ran while one was open for 31% -> 31% of each run, Pallas kernels for 0% -> 0%
where the time goes in v1:
time: 1550 us; the launch traced here: 1540 us
  blocking collectives  569 us (37%)
  waiting for transfers between devices  398 us (26%)
  matrix products  301 us (19%)
  local copies, waits for them, and re-layouts  113 us (7%)
  other arithmetic  109 us (7%)
  starting transfers between devices  24.5 us (2%)
  between operations  17.1 us (1%)
    psum x1, blocking collectives, shards(): lax.psum((owned_attn_gain, owned_query_w, owned_keyval_w, owned_query_gai...  294 us
    all_gather x1, blocking collectives, shards(): lax.all_gather(norm_ffn, 'dp', axis=0, tiled=True)  196 us
    reduce_scatter x1, waiting for transfers between devices, shards(): lax.psum_scatter(grad_down_part.astype(jnp.bfloat16), 'dp', scatter_dimen...  100 us
    reduce_scatter x1, waiting for transfers between devices, shards(): lax.psum_scatter(grad_up_part.astype(jnp.bfloat16), 'dp', scatter_dimensi...  100 us
    ppermute x3, waiting for transfers between devices, list_keys_on_mesh(): lax.ppermute(prior, 'dp', [(q, (q - o_now) % state_now) for q in range(st...  98.4 us
    reduce_scatter x1, waiting for transfers between devices, shards(): lax.psum_scatter(grad_gate_part.astype(jnp.bfloat16), 'dp', scatter_dimen...  71.4 us
    dot_general x4, matrix products, backward_block(): jnp.einsum('rkad,jkd->karj', grad_rows, value_rows, preferred_element_typ...  46 us
    convert_element_type x4, other arithmetic, backward_block(): grad_scores = (weights_full * (grad_weights - row_dot)).astype(jnp.bfloat16)  43.7 us
  transfers between devices with their start and end apart: 19, of which 7 were waited for; matrix products, arithmetic and copies ran while one was open for 31% of the time, Pallas kernels for 0%

profile of v1, /device:TPU:8, one launch (start us, length us, event | category | flops | bytes accessed | tf_op | source)
XLA Modules:
  0.0 1537.7 jit_solution(15737162873994259671)
XLA Ops:
  10.6 35.3 %all-gather = bf16[8,1,128]{2,1,0:T(2,128)(2,1)S(1)} all-gather(bf16[1,1,128]{2,1,0:T(2,128)(2,1)} %bitcast.336), channel_id=1, replica_groups=mesh['dp'=8,'seq'=4] {'dp'}, dimensions={0}, use_global_device_ids=true | all-gather | bytes 2304 | tf_op jit(solution)/shard_map/all_gather | solution.py:114
  49.6 14.9 all-reduce.8
  67.4 11.8 gather_fusion.1
  79.2 20.5 %gather_fusion = s32[2048]{0:T(1024)} fusion(s32[2048]{0:T(1024)S(1)} %bitcast.305, s32[2048]{0:T(1024)S(1)} %get-tuple-element.325), kind=kCustom, calls=%fused_computation | custom fusion | bytes 24576 | tf_op jit(solution)/shard_map/gather | solution.py:63
  114.2 4.3 all-to-all-start.1
  118.5 4.4 fusion.103
  127.2 4.6 all-to-all-done.1
  131.8 4.0 all-to-all-start
  135.8 98.4 %collective-permute-done.1 = bf16[1152,1024]{1,0:T(8,128)(2,1)} collective-permute-done((bf16[1152,1024]{1,0:T(8,128)(2,1)}, bf16[1152,1024]{1,0:T(8,128)(2,1)}, u32[]{:S(2)}, u32[]{:S(2)}) %collective-permute-start.1) | collective-permute-done | bytes 2359328 | tf_op jit(solution)/shard_map/ppermute | solution.py:206
  234.2 3.8 pad_maximum_fusion
  247.6 69.8 %while.28 = (s32[]{:T(128)}, bf16[4,512,2,2,64]{1,4,3,2,0:T(8,128)(2,1)}, f32[4,2,2,512,1]{3,2,1,4,0:T(2,128)}, s32[4]{0:T(128)S(1)}, s32[2048]{0:T(1024)}, /*in...) while((s32[]{:T(128)}, ...), condition=%wide.region_8.9_spmd.clone, body=%wide.region_5.8_spmd.clone.sunk | while | flops 1123155968 | bytes 56202504 | solution.py:189
  255.1 4.3 fusion.160
  260.1 5.0 fusion.161
  272.6 4.3 fusion.160
  277.5 5.0 fusion.161
  290.0 4.3 fusion.160
  295.0 5.0 fusion.161
  307.5 4.3 fusion.160
  312.4 5.0 fusion.161
  317.5 4.3 all-to-all-start.2
  321.7 195.9 %all-gather.1 = bf16[8,1,128]{2,1,0:T(2,128)(2,1)S(1)} all-gather(bf16[1,1,128]{2,1,0:T(2,128)(2,1)S(1)} %bitcast.337), channel_id=1, replica_groups=mesh['dp'=8,'seq'=4] {'dp'}, dimensions={0}, use_global_device_ids=true | all-gather | bytes 2304 | tf_op jit(solution)/shard_map/all_gather | solution.py:120
  530.5 5.1 constant_dynamic-update-slice_fusion.4
  541.1 5.1 constant_dynamic-update-slice_fusion
  546.2 11.4 fusion.106
  557.5 11.1 fusion.107
  568.7 17.4 %fusion.66 = (bf16[512,4608]{1,0:T(8,128)(2,1)}, bf16[512,4608]{1,0:T(8,128)(2,1)}, bf16[512,4608]{1,0:T(8,128)(2,1)}) fusion(f32[512,4608]{1,0:T(8,128)} %fusion.106, f32[512,4608]{1,0:T(8,128)} %fusion.107, bf16[512,1024]{1,0:T(8,128)(2,1)} %param.29, bf16[9216,1024]{1,0:T(8,128)(2,1)} %constant_dynamic-update-slice_fusion, s32[]{:T(128)S(6)} %select_n.60), kind=kOutput, calls=%fused_computation.75 | convolution fusion | flops 4869586944 | bytes 43515908 | tf_op jit(solution)/shard_map/dot_general | solution.py:71
  586.1 9.3 fusion.108
  595.8 5.9 multiply_reduce_fusion
  609.3 4.5 convolution_convert_fusion.3
  613.8 9.7 all-to-all-done.3
  628.9 210.6 %while.29 = (s32[]{:T(128)}, f32[2048,2,64]{0,2,1:T(8,128)}, f32[2048,2,64]{0,2,1:T(8,128)}, bf16[4,512,2,2,64]{1,4,3,2,0:T(8,128)(2,1)}, s32[4]{0:T(128)S(1)}, ...) while((s32[]{:T(128)}, f32[2048,2,64]{0,2,1:T(8,128)}, ...), condition=%wide.region_13.14_spmd.clone, body=%wide.region_11.13_spmd.clone.sunk | while | flops 2751987712 | bytes 288191712 | solution.py:280
  638.3 11.5 fusion.171
  649.8 10.9 fusion.172
  660.7 6.2 fusion.173
  666.9 7.5 fusion.175
  674.5 6.9 fusion.174
  690.3 11.5 fusion.171
  701.9 10.9 fusion.172
  712.8 6.4 fusion.173
  719.2 7.6 fusion.175
  726.8 7.2 fusion.174
  743.0 11.5 fusion.171
  754.5 10.9 fusion.172
  765.5 6.4 fusion.173
  771.9 7.5 fusion.175
  779.4 7.2 fusion.174
  795.7 11.5 fusion.171
  807.2 10.9 fusion.172
  818.1 6.4 fusion.173
  824.5 7.5 fusion.175
  832.1 7.2 fusion.174
  843.4 16.6 %all_to_all.90 = bf16[4,512,256]{1,2,0:T(8,128)(2,1)S(1)} all-to-all(bf16[4,512,256]{1,2,0:T(8,128)(2,1)S(1)} %copy.114), channel_id=1, replica_groups=mesh['dp'=8,'seq'=4] {'seq'}, dimensions={0} | all-to-all | bytes 2097152 | tf_op jit(solution)/shard_map/all_to_all | solution.py:293
  865.2 4.3 all-to-all-start.4
  871.7 10.0 all-to-all-done.4
  891.8 4.6 multiply_reduce_fusion.1
  899.2 10.0 convolution_convert_fusion.2
  909.2 10.3 convolution_convert_fusion.1
  920.7 10.0 convolution_convert_fusion
  932.3 9.9 add_convert_fusion
  948.8 12.5 all-reduce.7
  965.1 71.4 %reduce-scatter.13.cloned.1.call-done = bf16[1024,576]{0,1:T(8,128)(2,1)} async-done(((bf16[1024,4608]{0,1:T(8,128)(2,1)}), bf16[1024,576]{0,1:T(8,128)(2,1)}) %reduce-scatter.13.cloned.1.call-update) | async-done | bytes 1179664 | tf_op jit(solution)/shard_map/reduce_scatter | solution.py:232
  1036.5 100.0 %reduce-scatter.15.cloned.1.call-done = bf16[1024,576]{0,1:T(8,128)(2,1)} async-done(((bf16[1024,4608]{0,1:T(8,128)(2,1)}), bf16[1024,576]{0,1:T(8,128)(2,1)}) %reduce-scatter.15.cloned.1.call-update) | async-done | bytes 1179664 | tf_op jit(solution)/shard_map/reduce_scatter | solution.py:235
  1136.5 100.2 %reduce-scatter.17.cloned.1.call-done = bf16[576,1024]{1,0:T(8,128)(2,1)} async-done(((bf16[4608,1024]{1,0:T(8,128)(2,1)}), bf16[576,1024]{1,0:T(8,128)(2,1)}) %reduce-scatter.17.cloned.1.call-update) | async-done | bytes 1179664 | tf_op jit(solution)/shard_map/reduce_scatter | solution.py:238
  1236.7 294.2 %all-reduce.10 = (f32[128]{0:T(128)}, f32[128,1024]{1,0:T(8,128)}, f32[128,1024]{1,0:T(8,128)}, f32[8]{0:T(128)}, f32[8]{0:T(128)}, /*index=5*/f32[128,1024]{1,0...) all-reduce(f32[128]{0:T(128)S(1)} %dynamic-slice_convert_fusion.4, ...), channel_id=1, replica_groups=mesh['dp'=8,'seq'=4] {'seq'}, use_global_device_ids=true, to_apply=%region_19.20 | all-reduce | flops 2162960 | bytes 12978304 | tf_op jit(solution)/shard_map/psum | solution.py:366
  (367 shorter events, 167.5 us)
Async XLA Ops:
  7.2 100.7 %all-gather.10.cloned.1.call-start = ((), (), s32[]{:S(2)}) async-start(), calls=%async_computation.13 | async-start | bytes 2359296 | tf_op jit(solution)/shard_map/all_gather | solution.py:116
  7.9 110.5 %all-gather.8.cloned.1.call-start = ((), (), s32[]{:S(2)}) async-start(), calls=%async_computation.12 | async-start | bytes 2359296 | tf_op jit(solution)/shard_map/all_gather | solution.py:115
  8.7 515.8 %all-gather.12.cloned.1.call-start = ((), (), s32[]{:S(2)}) async-start(), calls=%async_computation.14 | async-start | bytes 2359296 | tf_op jit(solution)/shard_map/all_gather | solution.py:119
  9.4 536.8 %all-gather.14.cloned.1.call-start = ((), (), s32[]{:S(2)}) async-start(), calls=%async_computation.15 | async-start | bytes 10616832 | tf_op jit(solution)/shard_map/all_gather | solution.py:215
  10.0 547.6 %all-gather.16.cloned.1.call-start = ((), (), s32[]{:S(2)}) async-start(), calls=%async_computation.16 | async-start | bytes 10616832 | tf_op jit(solution)/shard_map/all_gather | solution.py:216
  10.0 92.3 %collective-permute-start = (bf16[576,1024]{1,0:T(8,128)(2,1)}, bf16[576,1024]{1,0:T(8,128)(2,1)S(1)}, u32[]{:S(2)}, u32[]{:S(2)}) collective-permute-start(bf16[576,1024]{1,0:T(8,128)(2,1)} %param.28), channel_id=1, source_target_pairs={{0,28},{4,0},{8,4},{12,8},{16,12},{20,16},{24,20},{28,24},{1,29},{... | collective-permute-start | bytes 3538952 | tf_op jit(solution)/shard_map/ppermute | solution.py:206
  45.8 72.6 %copy-start.39 = (f32[8,1,128]{2,1,0:T(1,128)}, f32[8,1,128]{2,1,0:T(1,128)S(1)}, u32[]{:S(2)}) copy-start(f32[8,1,128]{2,1,0:T(1,128)S(1)} %convert_element_type.218) | copy-start | bytes 12292
  64.5 46.9 %copy-start.43 = (f32[64]{0:T(128)}, f32[64]{0:T(128)S(1)}, u32[]{:S(2)}) copy-start(f32[64]{0:T(128)S(1)} %convert_element_type.177) | copy-start | bytes 772
  67.2 57.9 %copy-start.45 = (f32[64]{0:T(128)}, f32[64]{0:T(128)S(1)}, u32[]{:S(2)}) copy-start(f32[64]{0:T(128)S(1)} %convert_element_type.174) | copy-start | bytes 772
  67.4 11.8 copy-start
  79.2 23.1 %copy-start.9 = (bf16[576,1024]{1,0:T(8,128)(2,1)S(1)}, bf16[576,1024]{1,0:T(8,128)(2,1)}, u32[]{:S(2)}) copy-start(bf16[576,1024]{1,0:T(8,128)(2,1)} %param.28) | copy-start | bytes 3538948
  101.4 17.1 %copy-start.41 = (f32[512]{0:T(512)}, f32[512]{0:T(512)S(1)}, u32[]{:S(2)}) copy-start(f32[512]{0:T(512)S(1)} %add_rsqrt_fusion.3) | copy-start | bytes 6148
  102.3 23.3 %copy-start.25 = (f32[512,32]{0,1:T(8,128)}, f32[512,32]{0,1:T(8,128)S(1)}, u32[]{:S(2)}) copy-start(f32[512,32]{0,1:T(8,128)S(1)} %get-tuple-element.315) | copy-start | bytes 196612
  102.3 8.8 copy-start.10
  104.1 130.1 %collective-permute-start.1 = (bf16[1152,1024]{1,0:T(8,128)(2,1)}, bf16[1152,1024]{1,0:T(8,128)(2,1)}, u32[]{:S(2)}, u32[]{:S(2)}) collective-permute-start(bf16[1152,1024]{1,0:T(8,128)(2,1)} %pad_maximum_fusion.1), channel_id=1, source_target_pairs={{0,24},{4,28},{8,0},{12,4},{16,8},{20,12},{24,16},{28,20},{1,25},{... | collective-permute-start | bytes 7077896 | tf_op jit(solution)/shard_map/ppermute | solution.py:206
  111.4 7.1 copy-start.19
  114.2 17.7 %all-to-all-start.1 = ((bf16[512,4,256]{0,2,1:T(8,128)(2,1)}), bf16[512,4,256]{0,2,1:T(8,128)(2,1)}, u32[]{:S(2)}, u32[]{:S(2)}) async-start(bf16[512,4,256]{0,2,1:T(8,128)(2,1)} %bitcast.17), calls=%async_computation.1 | async-start | bytes 2097152 | tf_op jit(solution)/shard_map/all_to_all | solution.py:151
  131.8 111.1 %all-to-all-start = ((bf16[512,4,256]{0,2,1:T(8,128)(2,1)}), bf16[512,4,256]{0,2,1:T(8,128)(2,1)S(1)}, u32[]{:S(2)}, u32[]{:S(2)}) async-start(bf16[512,4,256]{0,2,1:T(8,128)(2,1)} %bitcast.11), calls=%async_computation | async-start | bytes 2097152 | tf_op jit(solution)/shard_map/all_to_all | solution.py:144
  238.0 292.5 %collective-permute-start.2 = (bf16[2304,1024]{1,0:T(8,128)(2,1)}, bf16[2304,1024]{1,0:T(8,128)(2,1)}, u32[]{:S(2)}, u32[]{:S(2)}) collective-permute-start(bf16[2304,1024]{1,0:T(8,128)(2,1)} %pad_maximum_fusion), channel_id=1, source_target_pairs={{0,16},{4,20},{8,24},{12,28},{16,0},{20,4},{24,8},{28,12},{1,17},{... | collective-permute-start | bytes 14155784 | tf_op jit(solution)/shard_map/ppermute | solution.py:206
  247.6 74.1 %copy-start.48 = (bf16[128]{0:T(256)(128)(2,1)S(1)}, bf16[128]{0:T(256)(128)(2,1)}, u32[]{:S(2)}) copy-start(bf16[128]{0:T(256)(128)(2,1)} %param.25) | copy-start | bytes 772
  317.5 207.0 %all-to-all-start.2 = ((bf16[4,512,256]{1,2,0:T(8,128)(2,1)}), bf16[4,512,256]{1,2,0:T(8,128)(2,1)}, u32[]{:S(2)}, u32[]{:S(2)}) async-start(bf16[4,512,256]{1,2,0:T(8,128)(2,1)} %bitcast.320), calls=%async_computation.2 | async-start | bytes 2097152 | tf_op jit(solution)/shard_map/all_to_all | solution.py:190
  586.1 9.4 copy-start.13
  586.1 9.4 copy-start.51
  586.1 9.8 copy-start.55
  605.7 17.8 %all-to-all-start.3 = ((bf16[512,4,256]{2,0,1:T(8,128)(2,1)}), bf16[512,4,256]{2,0,1:T(8,128)(2,1)S(1)}, u32[]{:S(2)}, u32[]{:S(2)}) async-start(bf16[512,4,256]{2,0,1:T(8,128)(2,1)} %bitcast.319), calls=%async_computation.3 | async-start | bytes 2097152 | tf_op jit(solution)/shard_map/all_to_all | solution.py:248
  609.2 355.9 %reduce-scatter.11.cloned.1.call-start = ((), (), s32[]{:S(2)}) async-start(), calls=%async_computation.19 | async-start | bytes 2359296 | tf_op jit(solution)/shard_map/reduce_scatter | solution.py:348
  613.8 351.3 %reduce-scatter.9.cloned.1.call-start = ((), (), s32[]{:S(2)}) async-start(), calls=%async_computation.18 | async-start | bytes 2359296 | tf_op jit(solution)/shard_map/reduce_scatter | solution.py:339
  637.5 12.3 copy-start.1
  660.7 13.7 copy-start.2
  674.5 6.9 copy-start.16
  674.5 6.9 copy-start.54
  689.6 12.3 copy-start.1
  712.8 14.0 copy-start.2
  726.8 7.3 copy-start.4
  726.8 7.3 copy-start.8
  726.8 7.3 copy-start.16
  726.8 7.3 copy-start.54
  742.2 12.3 copy-start.1
  765.4 14.0 copy-start.2
  779.4 7.3 copy-start.4
  779.4 7.3 copy-start.8
  779.4 7.3 copy-start.16
  779.4 7.3 copy-start.54
  794.9 12.3 copy-start.1
  818.1 14.0 copy-start.2
  832.1 7.3 copy-start.4
  832.1 7.3 copy-start.8
  832.1 7.3 copy-start.16
  832.1 7.3 copy-start.54
  842.3 17.9 %copy-start.26 = (f32[512,32]{0,1:T(8,128)S(1)}, f32[512,32]{0,1:T(8,128)}, u32[]{:S(2)}) copy-start(f32[512,32]{0,1:T(8,128)} %copy-done.25) | copy-start | bytes 196612
  842.3 17.9 %copy-start.34 = (f32[512,32]{0,1:T(8,128)S(1)}, f32[512,32]{0,1:T(8,128)}, u32[]{:S(2)}) copy-start(f32[512,32]{0,1:T(8,128)} %get-tuple-element.313) | copy-start | bytes 196612
  843.1 17.2 %copy-start.18 = (f32[512,1024]{0,1:T(8,128)S(1)}, f32[512,1024]{0,1:T(8,128)}, u32[]{:S(2)}) copy-start(f32[512,1024]{0,1:T(8,128)} %copy-done.17) | copy-start | bytes 6291460
  843.1 17.2 %copy-start.38 = (f32[512,8]{0,1:T(8,128)S(1)}, f32[512,8]{0,1:T(8,128)}, u32[]{:S(2)}) copy-start(f32[512,8]{0,1:T(8,128)} %copy-done.37) | copy-start | bytes 49156
  843.2 17.2 %copy-start.44 = (f32[64]{0:T(128)S(1)}, f32[64]{0:T(128)}, u32[]{:S(2)}) copy-start(f32[64]{0:T(128)} %copy-done.43) | copy-start | bytes 772
  862.3 7.2 copy-start.50
  862.3 7.3 copy-start.36
  865.2 16.5 %all-to-all-start.4 = ((bf16[4,512,256]{1,2,0:T(8,128)(2,1)}), bf16[4,512,256]{1,2,0:T(8,128)(2,1)}, u32[]{:S(2)}, u32[]{:S(2)}) async-start(bf16[4,512,256]{1,2,0:T(8,128)(2,1)} %bitcast.29), calls=%async_computation.4 | async-start | bytes 2097152 | tf_op jit(solution)/shard_map/all_to_all | solution.py:292
  869.4 95.6 %reduce-scatter.7.cloned.1.call-start = ((), (), s32[]{:S(2)}) async-start(), calls=%async_computation.17 | async-start | bytes 2359296 | tf_op jit(solution)/shard_map/reduce_scatter | solution.py:336
  871.7 11.8 copy-start.6
  871.7 11.8 copy-start.46
  899.1 137.4 %reduce-scatter.13.cloned.1.call-start = ((), (), s32[]{:S(2)}) async-start(), calls=%async_computation.20 | async-start | bytes 10616832 | tf_op jit(solution)/shard_map/reduce_scatter | solution.py:232
  909.2 227.4 %reduce-scatter.15.cloned.1.call-start = ((), (), s32[]{:S(2)}) async-start(), calls=%async_computation.21 | async-start | bytes 10616832 | tf_op jit(solution)/shard_map/reduce_scatter | solution.py:235
  919.5 317.2 %reduce-scatter.17.cloned.1.call-start = ((), (), s32[]{:S(2)}) async-start(), calls=%async_computation.22 | async-start | bytes 10616832 | tf_op jit(solution)/shard_map/reduce_scatter | solution.py:238
  945.7 15.9 %copy-start.23 = (f32[512,1024]{1,0:T(8,128)S(1)}, f32[512,1024]{1,0:T(8,128)}, u32[]{:S(2)}) copy-start(f32[512,1024]{1,0:T(8,128)} %copy-done.22) | copy-start | bytes 6291460
  (41 other events, 140.2 us)
Sparse Core Ops, SparseCore 0:
  9.6 36.7 all-gather.9
  48.0 30.1 all-gather.7
  79.8 28.6 all-gather.11
  109.9 126.8 all-gather.13
  238.3 215.4 all-gather.15
  613.9 33.6 reduce-scatter.10
  865.3 31.5 reduce-scatter.8
  899.7 34.7 reduce-scatter.6
  936.8 99.5 reduce-scatter.12
  1038.6 97.8 reduce-scatter.14
  1138.8 97.8 reduce-scatter.16
